TPU v7x, 32 devices: a whole 2x2x4 slice. The times are simulated.
32 devices in a mesh: groups: 2 (over x), seq: 16 (over z, y, core).
Axes of the slice: x: 2, y: 2, z: 4, core: 2. Of those that a mesh axis runs over, the one named last changes fastest.
Arguments:
- query_rows: bfloat16 [8192, 2048], P(('groups', 'seq')), parts along dimension 0, may hold values from -6 to 6
- key_rows: bfloat16 [16384, 2048], P(('groups', 'seq')), parts along dimension 0, may hold values from -6 to 6
- value_rows: bfloat16 [16384, 2048], P(('groups', 'seq')), parts along dimension 0, may hold values from -6 to 6
- write_rate: float32 [16384, 16], P(('groups', 'seq')), parts along dimension 0, may hold values from 0 to 1
- log_gate: float32 [8192, 16], P(('groups', 'seq')), parts along dimension 0, may hold values from -1 to 0
- keep_mask: int32 [256, 4], P(('groups', 'seq')), parts along dimension 0, may hold values 0 or 1
- query_kernel: float32 [4, 2048], replicated, may hold values from -3 to 3
- key_kernel: float32 [4, 2048], replicated, may hold values from -3 to 3
- value_kernel: float32 [4, 2048], replicated, may hold values from -3 to 3
Outputs:
- head_outputs: bfloat16 [8192, 2048], P(('groups', 'seq')), parts along dimension 0
There are 2 independent parts, one for each index of `groups`. A program takes and returns all parts, laid end to end along the dimension named above; an argument that names none is the same for every part. Nothing has to cross between parts.
All inputs are finite; a program needn't handle non-finite values. No bound on the sum of `keep_mask` on one device may be relied on, other than what follows from the above.
Results may differ from a plain program's by a relative error of at most 0.001.
Values may be sent and summed in bfloat16 or wider, within the bound.
No kernel may reach another device: no remote copies, remote signals or barrier semaphores. Data moves between devices by JAX's collectives and lax.ppermute only.
A program may use at most 128 MiB of HBM per device.

v0:
```python
import functools

import jax
import jax.numpy as jnp
from jax import lax
from jax.experimental import pallas as pl
from jax.experimental.pallas import tpu as pltpu
from jax.sharding import PartitionSpec as P

NH = 2
BLOCK = 16
SPAN = 64
DK = 128
CHUNK = 128
HALF = 64
PLANE = 4
PARTS = 2
HB = 2
READ_HB = 4
VMEM = 24 << 20
SMALL = pltpu.CompilerParams(vmem_limit_bytes=8 << 20)

WHOLE = pl.BlockSpec(memory_space=pltpu.VMEM)

F32 = jnp.float32
BF16 = jnp.bfloat16
NN = (((1,), (0,)), ((), ()))
NT = (((1,), (1,)), ((), ()))


def split(x):
    high = x.astype(BF16)
    low = (x - high.astype(F32)).astype(BF16)
    return high, low


def mm(a, b, dims=NN):
    return lax.dot_general(a, b, dims, preferred_element_type=F32)


def mm3(a, b):
    ah, al = a
    bh, bl = b
    return mm(jnp.concatenate([ah, al], axis=1), jnp.concatenate([bh, bh], axis=0)) + mm(ah, bl)


def mm3_nt(a, b):
    ah, al = a
    bh, bl = b
    return mm(jnp.concatenate([ah, al], axis=1), jnp.concatenate([bh, bh], axis=1), NT) + mm(ah, bl, NT)


def halves(x):
    left = iota(x.shape, 1) < HALF
    zero = jnp.zeros_like(x)
    return jnp.concatenate([jnp.where(left, x, zero), jnp.where(left, zero, x)], axis=0)


def pair_product(x, y):
    return mm3(x, (halves(y[0]), halves(y[1])))


def silu(v):
    return v / (1.0 + jnp.exp(-v))


def load_rows(scratch, rows_ref, lanes, tail):
    before = jnp.concatenate([jnp.zeros((13, tail.shape[1]), F32), tail.astype(F32)], axis=0)
    scratch[0:16, :] = before.astype(BF16)
    scratch[16 : 16 + rows_ref.shape[0], :] = rows_ref[:, lanes]


def shifter():
    shape = (3 * HALF, HALF + 16)
    row, col = iota(shape, 0), iota(shape, 1)
    return (col == 15 + row % HALF - row // HALF).astype(F32).astype(BF16)


def conv(shifts, scratch, kernel_ref, start, count):
    parts = []
    for at in range(start, start + count, HALF):
        moved = mm(shifts, scratch[at : at + HALF + 16, :])
        total = kernel_ref[3:4, :] * scratch[at + 16 : at + 16 + HALF, :].astype(F32)
        for back in range(1, 4):
            total = total + kernel_ref[3 - back : 4 - back, :] * moved[(back - 1) * HALF : back * HALF]
        parts.append(silu(total))
    return jnp.concatenate(parts, axis=0)


def unit(x):
    return x * lax.rsqrt(jnp.sum(x * x, axis=-1, keepdims=True) + 1e-06)


CORE, CHIP, GROUPS = 0, 1, 2
FLAGS = jax.ShapeDtypeStruct((8,), jnp.int32)
FLAGS_SPEC = pl.BlockSpec(memory_space=pltpu.SMEM)
TOKEN = pltpu.VMEM((8, 128), jnp.int32)


def hand_on(token_ref, token_out):
    token_out[...] = token_ref[...]


def lanes_at(flags_ref, which, at, group, heads=HB):
    first = flags_ref[GROUPS + which] * group + at * heads
    return pl.ds(pl.multiple_of(first * DK, heads * DK), heads * DK)


def in_hbm(x):
    return pltpu.with_memory_space_constraint(x, pltpu.HBM)


def held(x):
    return pltpu.with_memory_space_constraint(x, pltpu.VMEM)


def iota(shape, dim):
    return lax.broadcasted_iota(jnp.int32, shape, dim)


def prep_kernel(at_ref, rate_ref, log_ref, mask_ref, *refs):
    rows, outs, sems = refs[:3], refs[3:-1], refs[-1]
    rate_out, cum_out, row_out, read_out, flags_out, token_out = outs[:6]
    loads = [pltpu.make_async_copy(x, y, sems.at[i]) for i, (x, y) in enumerate(zip(rows, outs[6:]))]
    for load in loads:
        load.start()
    token_out[...] = jnp.zeros_like(token_out)
    place = lax.rem(at_ref[0], PLANE)
    flags_out[CORE] = lax.rem(place, 2)
    flags_out[CHIP] = lax.div(place, 2)
    for i, other in enumerate((3, 1, 2, 0)):
        flags_out[GROUPS + i] = place ^ other
    for i in range(GROUPS + PLANE, FLAGS.shape[0]):
        flags_out[i] = 0
    heads, steps = rate_ref.shape
    tokens = log_ref.shape[1]
    group = heads // PLANE
    subs, blocks = mask_ref.shape
    row_of = (iota((steps, blocks), 0) // SPAN == iota((steps, blocks), 1)).astype(F32)
    picked = mm(row_of, mask_ref[...].astype(F32), NT)
    sub_of = ((iota((steps, subs), 0) % SPAN) // BLOCK == iota((steps, subs), 1)).astype(F32)
    keep = jnp.sum(picked * sub_of, axis=1, keepdims=True)
    rates = rate_ref[...].T * keep
    turned = log_ref[...]
    logs = turned.T
    window = CHUNK // NH

    def upto(token, last):
        return ((token // window == last // window) & (token <= last)).astype(F32)

    high = lax.Precision.HIGHEST
    cum = jnp.dot(
        upto(iota((steps, tokens), 1), iota((steps, tokens), 0) // NH), logs, precision=high, preferred_element_type=F32
    )
    read = jnp.dot(
        upto(iota((tokens, tokens), 1), iota((tokens, tokens), 0)), logs, precision=high, preferred_element_type=F32
    )
    row = jnp.dot(
        turned,
        upto(iota((tokens, steps), 0), iota((tokens, steps), 1) // NH),
        precision=high,
        preferred_element_type=F32,
    )
    for g in range(PLANE):
        rate_out[g] = rates[:, g * group : (g + 1) * group]
        cum_out[g] = cum[:, g * group : (g + 1) * group]
        read_out[g] = read[:, g * group : (g + 1) * group]
    for b in range(steps // CHUNK):
        row_out[:, b, :] = row[:, b * CHUNK : (b + 1) * CHUNK]
    for load in loads:
        load.wait()


def last_rows_kernel(query_ref, key_ref, value_ref, out_ref):
    for i, ref in enumerate((query_ref, key_ref, value_ref)):
        out_ref[3 * i : 3 * i + 3, :] = ref[...].astype(F32)[13:16].astype(BF16)


def last_rows(*arrays):
    width = arrays[0].shape[1]
    return pl.pallas_call(
        last_rows_kernel,
        grid=(1,),
        in_specs=[pl.BlockSpec((16, width), functools.partial(lambda at, i: (at, 0), x.shape[0] // 16 - 1)) for x in arrays],
        out_specs=pl.BlockSpec((9, width), lambda i: (0, 0)),
        out_shape=jax.ShapeDtypeStruct((9, width), BF16),
        compiler_params=SMALL,
        name="last_rows",
    )(*map(in_hbm, arrays))


def prep(at, write_rate, log_gate, keep_mask, *rows):
    steps, heads = write_rate.shape
    tokens = log_gate.shape[0]
    group = heads // PLANE
    return pl.pallas_call(
        prep_kernel,
        out_shape=(
            jax.ShapeDtypeStruct((PLANE, steps, group), F32),
            jax.ShapeDtypeStruct((PLANE, steps, group), F32),
            jax.ShapeDtypeStruct((heads, steps // CHUNK, CHUNK), F32),
            jax.ShapeDtypeStruct((PLANE, tokens, group), F32),
            FLAGS,
            TOKEN,
            *(pltpu.VMEM(x.shape, x.dtype) for x in rows),
        ),
        in_specs=[FLAGS_SPEC] + [WHOLE] * 3 + [pl.BlockSpec(memory_space=pltpu.HBM)] * 3,
        out_specs=[WHOLE] * 4 + [FLAGS_SPEC] + [WHOLE] * 4,
        scratch_shapes=[pltpu.SemaphoreType.DMA((3,))],
        compiler_params=pltpu.CompilerParams(vmem_limit_bytes=VMEM),
        name="prep",
    )(at, write_rate.T, log_gate.T, keep_mask.T, *(pltpu.with_memory_space_constraint(x, pltpu.HBM) for x in rows))


def block_inverses(lowers, fill):
    row = iota((HALF, CHUNK), 0)
    col = iota((HALF, CHUNK), 1) % HALF
    eye = (row == col).astype(F32)
    near = row // BLOCK == col // BLOCK
    inner = [jnp.where(near, -x, 0.0) for x in lowers]
    outer = [split(jnp.where(near, 0.0, x)) for x in lowers]
    power = [split(x) for x in inner]
    a = [eye + x for x in inner]
    for _ in range(3):
        fill()
        power = [split(pair_product(x, x)) for x in power]
        fill()
        a = [x + pair_product(split(x), y) for x, y in zip(a, power)]
    sa = [split(x) for x in a]
    fill()
    m = [split(pair_product(x, y)) for x, y in zip(sa, outer)]
    fill()
    m2 = [split(pair_product(x, x)) for x in m]
    t = [x - pair_product(y, z) for x, y, z in zip(a, m, sa)]
    return [x + pair_product(y, split(x)) for x, y in zip(t, m2)]


def maps_kernel(
    which,
    flags_ref,
    key_ref,
    value_ref,
    tail_ref,
    key_kernel_ref,
    value_kernel_ref,
    rate_ref,
    cum_ref,
    row_ref,
    token_ref,
    map_out,
    wh_out,
    wl_out,
    mh_out,
    ml_out,
    token_out,
    scratch,
    value_scratch,
):
    hand_on(token_ref, token_out)
    steps = key_ref.shape[0]
    chunks = steps // CHUNK
    at = pl.program_id(0)
    lanes = lanes_at(flags_ref, which, at, rate_ref.shape[2])
    load_rows(scratch, key_ref, lanes, tail_ref[3:6, :])
    load_rows(value_scratch, value_ref, lanes, tail_ref[6:9, :])
    shifts = shifter()
    keys = conv(shifts, scratch, key_kernel_ref, 0, steps)
    keys = jnp.concatenate([unit(keys[:, h * DK : (h + 1) * DK]) for h in range(HB)], axis=1)
    kh, kl = split(keys)
    group = rate_ref.shape[2]
    rates, cums = rate_ref[0], cum_ref[0]

    def column(x, h):
        out = x[:, h : h + 1]
        for turn in range(1, group // HB):
            out = jnp.where(at == turn, x[:, turn * HB + h : turn * HB + h + 1], out)
        return out

    below = iota((CHUNK, CHUNK), 1) < iota((CHUNK, CHUNK), 0)
    left = iota((HALF, CHUNK), 1) < HALF
    items = [(h, c) for h in range(HB) for c in range(chunks)]
    columns = [(column(rates, h), column(cums, h)) for h in range(HB)]
    lowers, crosses, sides, faded, ends = [], [], {}, {}, {}
    for h, c in items:
        lanes = slice(h * DK, (h + 1) * DK)
        rows = slice(c * CHUNK, (c + 1) * CHUNK)
        row_c = row_ref[h, c : c + 1, :]
        rate_c, cum_c = (x[rows] for x in columns[h])
        mine = (kh[rows, lanes], kl[rows, lanes])
        decay = jnp.exp(jnp.where(below, cum_c - row_c, 0.0))
        lower = jnp.where(below, rate_c * decay * mm3_nt(mine, mine), 0.0)
        lowers.append(jnp.where(left, lower[:HALF], lower[HALF:]))
        crosses.append(split(jnp.where(left, lower[HALF:], 0.0)))

    def side(c):
        rows = slice(c * CHUNK, (c + 1) * CHUNK)
        values = conv(shifts, value_scratch, value_kernel_ref, c * CHUNK, CHUNK)
        for h in range(HB):
            lanes = slice(h * DK, (h + 1) * DK)
            rate_c, cum_c = (x[rows] for x in columns[h])
            grown = rate_c * jnp.exp(cum_c) * keys[rows, lanes]
            sides[h, c] = split(jnp.concatenate([grown, rate_c * values[:, lanes]], axis=1))

    def fade(c):
        for h in range(HB):
            row_c = row_ref[h, c : c + 1, :]
            end = row_c[:, CHUNK - 1 : CHUNK]
            k_c = keys[c * CHUNK : (c + 1) * CHUNK, h * DK : (h + 1) * DK]
            faded[h, c] = split(k_c.T * jnp.exp(end - row_c))
            ends[h, c] = jnp.exp(end)

    todo = [functools.partial(f, c) for c in range(chunks) for f in (side, fade)]

    def fill():
        if todo:
            todo.pop(0)()

    eye = (iota((DK, DK), 0) == iota((DK, DK), 1)).astype(F32)
    inverses = block_inverses(lowers, fill)
    while todo:
        fill()
    pieces = [split(x) for x in inverses]
    under = [mm3(y, tuple(jnp.concatenate([z, z], axis=0) for z in x)) for x, y in zip(pieces, crosses)]
    under = [split(jnp.where(left, x, 0.0)) for x in under]
    under = [
        mm3(x, tuple(jnp.concatenate([jnp.zeros_like(z), z], axis=0) for z in y)) for x, y in zip(pieces, under)
    ]
    whole = [
        split(jnp.concatenate([jnp.where(left, x, 0.0), jnp.where(left, -y, x)], axis=0))
        for x, y in zip(inverses, under)
    ]
    solved = [split(mm3(x, sides[i])) for i, x in zip(items, whole)]
    for (h, c), x in zip(items, solved):
        at_w = slice(c * CHUNK, (c + 1) * CHUNK)
        wh_out[at * HB + h, at_w, :], wl_out[at * HB + h, at_w, :] = x
    made = [mm3(faded[i], x) for i, x in zip(items, solved)]
    made = [jnp.concatenate([ends[i] * eye - x[:, :DK], x[:, DK:]], axis=1) for i, x in zip(items, made)]

    def then(late, early):
        both = mm3(split(late[:, :DK]), early)
        return jnp.concatenate([both[:, :DK], both[:, DK:] + late[:, DK:]], axis=1)

    assert chunks == 4
    heads = range(HB)
    first, third = ([split(made[h * chunks + c]) for h in heads] for c in (0, 2))
    two = [split(then(made[h * chunks + 1], first[h])) for h in heads]
    last = [then(made[h * chunks + 3], third[h]) for h in heads]
    last = [then(last[h], two[h]) for h in heads]
    for h in heads:
        map_out[at * HB + h] = last[h]
        for i, x in enumerate((first[h], two[h], third[h])):
            at_m = slice(i * DK, (i + 1) * DK)
            mh_out[at * HB + h, at_m, :], ml_out[at * HB + h, at_m, :] = x


def group_maps(flags, token, which, key_rows, value_rows, tails, key_kernel, value_kernel, scalars):
    rate_cols, cum_cols, chunk_rows, _ = scalars
    steps, width = key_rows.shape
    heads = width // DK
    group = heads // PLANE
    turns = group // HB
    lanes = HB * DK
    chunks = steps // CHUNK

    def wide(i, g):
        return (0, g[GROUPS + which] * turns + i)

    def per_head(i, g):
        return (g[GROUPS + which] * turns + i, 0, 0)

    return pl.pallas_call(
        functools.partial(maps_kernel, which),
        grid_spec=pltpu.PrefetchScalarGridSpec(
            num_scalar_prefetch=1,
            grid=(turns,),
            in_specs=[
                WHOLE,
                WHOLE,
                pl.BlockSpec((tails.shape[0], lanes), wide),
                pl.BlockSpec((4, lanes), wide),
                pl.BlockSpec((4, lanes), wide),
                pl.BlockSpec((1, steps, group), lambda i, g: (g[GROUPS + which], 0, 0)),
                pl.BlockSpec((1, steps, group), lambda i, g: (g[GROUPS + which], 0, 0)),
                pl.BlockSpec((HB, chunks, CHUNK), per_head),
                WHOLE,
            ],
            out_specs=[
                WHOLE,
                WHOLE,
                WHOLE,
                WHOLE,
                WHOLE,
                WHOLE,
            ],
            scratch_shapes=[pltpu.VMEM((steps + 16, lanes), BF16)] * 2,
        ),
        out_shape=(
            pltpu.VMEM((group, DK, 2 * DK), F32),
            pltpu.VMEM((group, steps, 2 * DK), BF16),
            pltpu.VMEM((group, steps, 2 * DK), BF16),
            pltpu.VMEM((group, 3 * DK, 2 * DK), BF16),
            pltpu.VMEM((group, 3 * DK, 2 * DK), BF16),
            TOKEN,
        ),
        compiler_params=pltpu.CompilerParams(vmem_limit_bytes=VMEM),
        name="maps",
    )(flags, key_rows, value_rows, tails, key_kernel, value_kernel, rate_cols, cum_cols, chunk_rows, held(token))


def reads_kernel(
    which,
    flags_ref,
    query_ref,
    tail_ref,
    query_kernel_ref,
    key_ref,
    key_kernel_ref,
    read_ref,
    row_ref,
    wh_ref,
    wl_ref,
    mh_ref,
    ml_ref,
    token_ref,
    qh_out,
    ql_out,
    own_out,
    token_out,
    scratch,
    key_scratch,
):
    hand_on(token_ref, token_out)
    tokens = query_ref.shape[0]
    window = CHUNK // NH
    chunks = tokens // window
    at = pl.program_id(0)
    lanes = lanes_at(flags_ref, which, at, read_ref.shape[2], READ_HB)
    load_rows(scratch, query_ref, lanes, tail_ref[0:3, :])
    shifts = shifter()
    queries = conv(shifts, scratch, query_kernel_ref, 0, tokens)
    queries = jnp.concatenate([unit(queries[:, h * DK : (h + 1) * DK]) for h in range(READ_HB)], axis=1)
    load_rows(key_scratch, key_ref, lanes, tail_ref[3:6, :])
    keys = conv(shifts, key_scratch, key_kernel_ref, 0, NH * tokens)
    group = read_ref.shape[2]
    reads = read_ref[0]
    visible = iota((window, CHUNK), 1) <= NH * iota((window, CHUNK), 0) + NH - 1
    items = [(h, c) for h in range(READ_HB) for c in range(chunks)]
    pieces, columns, lifted = [], [], []
    for h in range(READ_HB):
        lanes = slice(h * DK, (h + 1) * DK)
        read_h = reads[:, h : h + 1]
        for turn in range(1, group // READ_HB):
            read_h = jnp.where(at == turn, reads[:, turn * READ_HB + h : turn * READ_HB + h + 1], read_h)
        columns.append(read_h)
        lifted.append(jnp.exp(read_h) * queries[:, lanes])
        pieces.append((split(queries[:, lanes]), split(unit(keys[:, lanes]))))

    def tokens_of(c):
        return slice(c * window, (c + 1) * window)

    def steps_of(c):
        return slice(c * CHUNK, (c + 1) * CHUNK)

    scores = [
        mm3_nt(tuple(x[tokens_of(c)] for x in pieces[h][0]), tuple(x[steps_of(c)] for x in pieces[h][1]))
        for h, c in items
    ]
    starts = {}
    for h in range(READ_HB):
        kept = [tuple(x[at * READ_HB + h, i * DK : (i + 1) * DK, :] for x in (mh_ref, ml_ref)) for i in range(3)]
        first, two, third = kept
        three = mm3(tuple(x[:, :DK] for x in third), two)
        late = third[0][:, DK:].astype(F32) + third[1][:, DK:].astype(F32)
        three = split(jnp.concatenate([three[:, :DK], three[:, DK:] + late], axis=1))
        starts[h] = [None, first, two, three]
    inner = []
    for (h, c), x in zip(items, scores):
        spread = columns[h][tokens_of(c)] - row_ref[h, c : c + 1, :]
        inner.append(split(jnp.where(visible, jnp.exp(jnp.where(visible, spread, 0.0)) * x, 0.0)))
    solved = [tuple(x[at * READ_HB + h, steps_of(c), :] for x in (wh_ref, wl_ref)) for h, c in items]
    got = [mm3(x, y) for x, y in zip(inner, solved)]
    eff = [lifted[h][tokens_of(c)] - x[:, :DK] for (h, c), x in zip(items, got)]
    eff_pieces = [split(x) for x in eff]
    taken = [None if c == 0 else mm3(x, starts[h][c]) for (h, c), x in zip(items, eff_pieces)]
    for (h, c), x, y, z in zip(items, eff_pieces, got, taken):
        at_out = (at * READ_HB + h, tokens_of(c))
        qh_out[at_out], ql_out[at_out] = x if c == 0 else split(z[:, :DK])
        own_out[at_out] = y[:, DK:] if c == 0 else y[:, DK:] + z[:, DK:]


def group_reads(flags, token, which, query_rows, key_rows, tails, query_kernel, key_kernel, scalars, kept):
    _, _, chunk_rows, read_cols = scalars
    tokens, width = query_rows.shape
    steps = tokens * NH
    heads = width // DK
    group = heads // PLANE
    turns = group // READ_HB
    lanes = READ_HB * DK
    chunks = steps // CHUNK

    def wide(i, g):
        return (0, g[GROUPS + which] * turns + i)

    return pl.pallas_call(
        functools.partial(reads_kernel, which),
        grid_spec=pltpu.PrefetchScalarGridSpec(
            num_scalar_prefetch=1,
            grid=(turns,),
            in_specs=[
                WHOLE,
                pl.BlockSpec((tails.shape[0], lanes), wide),
                pl.BlockSpec((4, lanes), wide),
                WHOLE,
                pl.BlockSpec((4, lanes), wide),
                pl.BlockSpec((1, tokens, group), lambda i, g: (g[GROUPS + which], 0, 0)),
                pl.BlockSpec((READ_HB, chunks, CHUNK), lambda i, g: (g[GROUPS + which] * turns + i, 0, 0)),
                WHOLE,
                WHOLE,
                WHOLE,
                WHOLE,
                WHOLE,
            ],
            out_specs=[WHOLE] * 4,
            scratch_shapes=[pltpu.VMEM((tokens + 16, lanes), BF16), pltpu.VMEM((steps + 16, lanes), BF16)],
        ),
        out_shape=(
            pltpu.VMEM((group, tokens, DK), BF16),
            pltpu.VMEM((group, tokens, DK), BF16),
            pltpu.VMEM((group, tokens, DK), F32),
            TOKEN,
        ),
        compiler_params=pltpu.CompilerParams(vmem_limit_bytes=VMEM),
        name="reads",
    )(flags, query_rows, tails, query_kernel, key_rows, key_kernel, read_cols, chunk_rows, *map(held, kept), held(token))


def small(kernel, flags, token, operands, outs, name):
    def whole(shape):
        return pl.BlockSpec(shape, lambda i, f: (0,) * len(shape))

    def body(flags_ref, token_ref, *refs):
        hand_on(token_ref, refs[-1])
        kernel(flags_ref, *refs[:-1])

    return pl.pallas_call(
        body,
        grid_spec=pltpu.PrefetchScalarGridSpec(
            num_scalar_prefetch=1,
            grid=(1,),
            in_specs=[WHOLE] + [whole(x.shape) for x in operands],
            out_specs=[whole(shape) for shape in outs] + [WHOLE],
        ),
        out_shape=[jax.ShapeDtypeStruct(shape, F32) for shape in outs] + [TOKEN],
        compiler_params=SMALL,
        name=name,
    )(flags, held(token), *operands)


def after(first, mine, other):
    early = jnp.where(first, mine, other)
    late = jnp.where(first, other, mine)
    both = mm3(split(late[:, :DK]), split(early))
    return jnp.concatenate([both[:, :DK], both[:, DK:] + late[:, DK:]], axis=1)


def compose_kernel(flags_ref, mine_ref, other_ref, out_ref):
    heads = range(mine_ref.shape[0])
    for h, x in enumerate([after(flags_ref[CORE] == 0, mine_ref[h], other_ref[h]) for h in heads]):
        out_ref[h] = x


def composed(flags, token, mine, other):
    return small(compose_kernel, flags, token, [mine, other], [mine.shape], "compose")


def plane_kernel(flags_ref, mine_ref, pair_ref, other_ref, chip_out, *outs):
    parts = len(outs) // 3
    for zero_out in outs[2 * parts :]:
        zero_out[...] = jnp.zeros_like(zero_out)
    heads = range(mine_ref.shape[0])
    chips = [after(flags_ref[CORE] == 0, mine_ref[h], pair_ref[h]) for h in heads]
    planes = [after(flags_ref[CHIP] == 0, chips[h], other_ref[h]) for h in heads]
    for h in heads:
        chip_out[h] = chips[h]
        part, at = h * parts // len(heads), h % (len(heads) // parts)
        outs[part][at] = planes[h]
        outs[parts + part][at] = planes[h][:, DK:]


def plane_composed(flags, token, mine, pair, other):
    part = mine.shape[0] // PARTS
    shapes = [(part, DK, 2 * DK)] * PARTS + [(part, DK, DK)] * (2 * PARTS)
    chip_map, *outs, token = small(plane_kernel, flags, token, [mine, pair, other], [mine.shape] + shapes, "plane")
    return chip_map, outs[:PARTS], outs[PARTS : 2 * PARTS], outs[2 * PARTS :], token


def apply_kernel(flags_ref, map_ref, held_ref, come_ref, state_out, exit_out):
    heads = range(map_ref.shape[0])
    state = [held_ref[h] + come_ref[h] for h in heads]
    got = [mm3(split(map_ref[h, :, :DK]), split(state[h])) for h in heads]
    for h in heads:
        state_out[h] = state[h]
        exit_out[h] = got[h] + map_ref[h, :, DK:]


def applied(flags, token, maps, state, come):
    return small(apply_kernel, flags, token, [maps, state, come], [state.shape] * 2, "apply")


def branches(first, mine, other, entry):
    heads = range(len(entry))
    early = [jnp.where(first, mine[h], other[h]) for h in heads]
    later = [mm3(split(early[h][:, :DK]), split(entry[h])) + early[h][:, DK:] for h in heads]
    own = [jnp.where(first, entry[h], later[h]) for h in heads]
    return own, [jnp.where(first, later[h], entry[h]) for h in heads]


def branch_kernel(flags_ref, mine_ref, other_ref, entry_ref, keep_out, send_out):
    refs = (mine_ref, other_ref, entry_ref)
    own, send = branches(flags_ref[CORE] == 0, *([x[h] for h in range(x.shape[0])] for x in refs))
    for h in range(len(own)):
        keep_out[h] = own[h]
        send_out[h] = send[h]


def branched(flags, token, mine, other, entry):
    return small(branch_kernel, flags, token, [mine, other, entry], [entry.shape] * 2, "branch")


def fork_kernel(flags_ref, chip_map_ref, from_chip_ref, map_ref, pair_ref, *refs):
    maps = (chip_map_ref, from_chip_ref, map_ref, pair_ref)
    chip_map, from_chip, mine, pair = ([x[h] for h in range(x.shape[0])] for x in maps)
    states, outs = refs[: 2 * PARTS], refs[2 * PARTS :]
    state, come = ([x[h] for x in part for h in range(x.shape[0])] for part in (states[:PARTS], states[PARTS:]))
    entry = [x + y for x, y in zip(state, come)]
    own, across = branches(flags_ref[CHIP] == 0, chip_map, from_chip, entry)
    for out_ref, states in zip(outs, (across, *branches(flags_ref[CORE] == 0, mine, pair, own))):
        for h, state in enumerate(states):
            out_ref[h] = state


def forked(flags, token, chip_map, from_chip, mine, pair, state, come):
    operands = [chip_map, from_chip, mine, pair, *state, *come]
    return small(fork_kernel, flags, token, operands, [(mine.shape[0], DK, DK)] * 3, "fork")


def finish_kernel(flags_ref, token_ref, qh_ref, ql_ref, own_ref, entry_ref, *refs):
    out_ref, token_out = refs[-2:]
    hand_on(token_ref, token_out)
    for h in range(entry_ref.shape[0]):
        lanes = slice(h * DK, (h + 1) * DK)
        got = mm3((qh_ref[h], ql_ref[h]), split(entry_ref[h]))
        out_ref[:, lanes] = (own_ref[h] + got).astype(BF16)


def finished(flags, token, which, read, entry, out, width):
    qh, ql, own, _ = read
    group, tokens, _ = qh.shape
    operands = [held(token), held(qh), held(ql), held(own), entry]
    specs = [WHOLE] * 4 + [pl.BlockSpec(entry.shape, lambda i, g: (0, 0, 0))]
    if out is not None:
        operands.append(out)
        specs.append(pl.BlockSpec(memory_space=pl.ANY))
    return pl.pallas_call(
        finish_kernel,
        grid_spec=pltpu.PrefetchScalarGridSpec(
            num_scalar_prefetch=1,
            grid=(1,),
            in_specs=specs,
            out_specs=[pl.BlockSpec((tokens, group * DK), lambda i, g: (0, g[GROUPS + which])), WHOLE],
        ),
        out_shape=[jax.ShapeDtypeStruct((tokens, width), BF16), TOKEN],
        input_output_aliases={} if out is None else {len(operands): 0},
        compiler_params=SMALL,
        name="finish",
    )(flags, *operands)


def moved(x, pairs):
    return pltpu.with_memory_space_constraint(lax.ppermute(x, "seq", pairs), pltpu.VMEM)


def local(
    count,
    query_rows,
    key_rows,
    value_rows,
    write_rate,
    log_gate,
    keep_mask,
    query_kernel,
    key_kernel,
    value_kernel,
):
    tails = moved(last_rows(query_rows, key_rows, value_rows), [(s, s + 1) for s in range(count - 1)])
    query_kernel, key_kernel, value_kernel = held(query_kernel), held(key_kernel), held(value_kernel)
    *scalars, flags, token, query_rows, key_rows, value_rows = prep(
        lax.axis_index("seq")[None], write_rate, log_gate, keep_mask, query_rows, key_rows, value_rows
    )
    query_rows, key_rows, value_rows = held(query_rows), held(key_rows), held(value_rows)
    pair = [(s, s ^ 1) for s in range(count)]
    across = [(s, s ^ 2) for s in range(count)]
    made, from_pair = {}, {}
    for i in (0, 2, 1, 3):
        *one, token = group_maps(flags, token, i, key_rows, value_rows, tails, key_kernel, value_kernel, scalars)
        made[i] = one
        if i < 2:
            from_pair[i] = moved(one[0], pair)
        if i == 2:
            next_map, token = composed(flags, token, one[0], from_pair[0])
            from_chip = moved(next_map, across)
    maps = [made[i][0] for i in range(PLANE)]
    chip_map, plane_maps, offset, state, token = plane_composed(flags, token, maps[3], from_pair[1], from_chip)

    def read(token, i):
        return group_reads(
            flags, token, i, query_rows, key_rows, tails, query_kernel, key_kernel, scalars, made[i][1:]
        )

    reads = []
    for i in range(count // PLANE - 1):
        if i > 0:
            offset = []
            for part in range(PARTS):
                state[part], part_offset, token = applied(flags, token, plane_maps[part], state[part], come[part])
                offset.append(part_offset)
        come = [moved(x, [(s, s + PLANE) for s in range(i * PLANE, (i + 1) * PLANE)]) for x in offset]
        if len(reads) < PLANE - 1:
            reads.append(read(token, i))
            token = reads[-1][-1]
    send, own_entry, own_send, token = forked(flags, token, chip_map, from_chip, maps[3], from_pair[1], state, come)
    theirs = moved(send, across)
    far_own = moved(own_send, pair)
    for i in range(len(reads), PLANE):
        reads.append(read(token, i))
        token = reads[-1][-1]
    width = query_rows.shape[1]
    out, token = finished(flags, token, 3, reads[3], own_entry, None, width)
    out, token = finished(flags, token, 1, reads[1], far_own, out, width)
    next_entry, next_send, token = branched(flags, token, maps[2], from_pair[0], theirs)
    far_next = moved(next_send, pair)
    out, token = finished(flags, token, 2, reads[2], next_entry, out, width)
    return finished(flags, token, 0, reads[0], far_next, out, width)[0]


def solution(mesh):
    rows = P(("groups", "seq"), None)
    return jax.shard_map(
        functools.partial(local, mesh.shape["seq"]),
        mesh=mesh,
        in_specs=(rows, rows, rows, rows, rows, rows, P(), P(), P()),
        out_specs=rows,
        check_vma=False,
    )
```

profile of v0, /device:TPU:9, one launch (start us, length us, event | category | flops | bytes accessed | tf_op | source)
XLA Modules:
  0.0 83.5 jit_solution(9383856620519861402)
XLA Ops:
  0.0 1.0 %last_rows.1 = bf16[9,2048]{1,0:T(8,128)(2,1)S(1)} custom-call(bf16[256,2048]{1,0:T(8,128)(2,1)} %query_ref.1, bf16[512,2048]{1,0:T(8,128)(2,1)} %key_ref.1, bf16[512,2048]{1,0:T(8,128)(2,1)} %value_ref.1), custom_call_target="tpu_custom_call" | custom-call | tf_op jit(solution)/shard_map/last_rows/pallas_call | solution.py:181
  1.0 3.7 %collective-permute-start = (bf16[9,2048]{1,0:T(8,128)(2,1)S(1)}, bf16[9,2048]{1,0:T(8,128)(2,1)S(1)}, u32[]{:S(2)}, u32[]{:S(2)}) collective-permute-start(bf16[9,2048]{1,0:T(8,128)(2,1)S(1)} %last_rows.1), channel_id=1, source_target_pairs={{0,1},{1,2},{2,3},{3,4},{4,5},{5,6},{6,7},{7,8},{8,9},{9,10},{10,1... | collective-permute-start | bytes 110600 | tf_op jit(solution)/shard_map/ppermute | solution.py:680
  4.7 0.0 copy-start
  4.7 0.0 copy-start.1
  4.8 3.2 %prep.1 = (f32[4,512,4]{2,1,0:T(8,128)S(1)}, f32[4,512,4]{2,1,0:T(8,128)S(1)}, f32[16,4,128]{2,1,0:T(4,128)S(1)}, f32[4,256,4]{2,1,0:T(8,128)S(1)}, s32[8]{0:T(1...) custom-call(s32[1]{0:T(128)} %bitcast.at_ref, ...), custom_call_target="tpu_custom_call" | custom-call | tf_op jit(solution)/shard_map/prep/pallas_call | solution.py:196
  7.9 0.0 collective-permute-done.tail_ref
  8.0 8.6 %maps.4 = (f32[4,128,256]{2,1,0:T(8,128)S(1)}, bf16[4,512,256]{2,1,0:T(8,128)(2,1)S(1)}, bf16[4,512,256]{2,1,0:T(8,128)(2,1)S(1)}, bf16[4,384,256]{2,1,0:T(8,128...) custom-call(s32[8]{0:T(128)S(1)} %get-tuple-element.90.flags_ref, ...), custom_call_target="tpu_custom_call" | custom-call | tf_op jit(solution)/shard_map/maps/pallas_call | solution.py:371
  16.6 0.3 collective-permute-start.1
  16.8 8.6 %maps.5 = (f32[4,128,256]{2,1,0:T(8,128)S(1)}, bf16[4,512,256]{2,1,0:T(8,128)(2,1)S(1)}, bf16[4,512,256]{2,1,0:T(8,128)(2,1)S(1)}, bf16[4,384,256]{2,1,0:T(8,128...) custom-call(s32[8]{0:T(128)S(1)} %get-tuple-element.90.flags_ref, ...), custom_call_target="tpu_custom_call" | custom-call | tf_op jit(solution)/shard_map/maps/pallas_call | solution.py:371
  25.4 0.0 collective-permute-done.1.refs_1_
  25.4 0.9 %compose.1 = (f32[4,128,256]{2,1,0:T(8,128)S(1)}, s32[8,128]{1,0:T(8,128)S(1)}) custom-call(s32[8]{0:T(128)S(1)} %get-tuple-element.90.flags_ref, s32[8,128]{1,0:T(8,128)S(1)} %get-tuple-element.100.token_ref, f32[4,128,256]{2,1,0:T(8,128)S(1)} %get-tuple-element.101.refs_0_, f32[4,128,256]{2,1,0:T(8,128)S(1)} %collective-permute-done.1.refs_1_), custom_call_target="tpu_custom_call" | custom-call | tf_op jit(solution)/shard_map/compose/pallas_call | solution.py:545
  26.3 1.2 %collective-permute-start.3 = (f32[4,128,256]{2,1,0:T(8,128)S(1)}, f32[4,128,256]{2,1,0:T(8,128)S(1)}, u32[]{:S(2)}, u32[]{:S(2)}) collective-permute-start(f32[4,128,256]{2,1,0:T(8,128)S(1)} %get-tuple-element.124), channel_id=1, source_target_pairs={{0,2},{1,3},{2,0},{3,1},{4,6},{5,7},{6,4},{7,5},{8,10},{9,11},{10,... | collective-permute-start | bytes 1572872 | tf_op jit(solution)/shard_map/ppermute | solution.py:680
  27.5 8.8 %maps.6 = (f32[4,128,256]{2,1,0:T(8,128)S(1)}, bf16[4,512,256]{2,1,0:T(8,128)(2,1)S(1)}, bf16[4,512,256]{2,1,0:T(8,128)(2,1)S(1)}, bf16[4,384,256]{2,1,0:T(8,128...) custom-call(s32[8]{0:T(128)S(1)} %get-tuple-element.90.flags_ref, ...), custom_call_target="tpu_custom_call" | custom-call | tf_op jit(solution)/shard_map/maps/pallas_call | solution.py:371
  36.2 0.8 collective-permute-start.2
  37.1 8.6 %maps.7 = (f32[4,128,256]{2,1,0:T(8,128)S(1)}, bf16[4,512,256]{2,1,0:T(8,128)(2,1)S(1)}, bf16[4,512,256]{2,1,0:T(8,128)(2,1)S(1)}, bf16[4,384,256]{2,1,0:T(8,128...) custom-call(s32[8]{0:T(128)S(1)} %get-tuple-element.90.flags_ref, ...), custom_call_target="tpu_custom_call" | custom-call | tf_op jit(solution)/shard_map/maps/pallas_call | solution.py:371
  45.7 0.0 collective-permute-done.3.refs_2_.refs_1_
  45.7 0.0 collective-permute-done.2.refs_1_.refs_3_
  45.7 1.1 %plane.1 = (f32[4,128,256]{2,1,0:T(8,128)S(1)}, f32[2,128,256]{2,1,0:T(8,128)S(1)}, f32[2,128,256]{2,1,0:T(8,128)S(1)}, f32[2,128,128]{2,1,0:T(8,128)S(1)}, f32[...) custom-call(s32[8]{0:T(128)S(1)} %get-tuple-element.90.flags_ref, ...), custom_call_target="tpu_custom_call" | custom-call | tf_op jit(solution)/shard_map/plane/pallas_call | solution.py:545
  46.8 1.3 %collective-permute-start.4 = (f32[2,128,128]{2,1,0:T(8,128)S(1)}, f32[2,128,128]{2,1,0:T(8,128)S(1)}, u32[]{:S(2)}, u32[]{:S(2)}) collective-permute-start(f32[2,128,128]{2,1,0:T(8,128)S(1)} %get-tuple-element.129), channel_id=1, source_target_pairs={{0,4},{1,5},{2,6},{3,7},{16,20},{17,21},{18,22},{19,23}} | collective-permute-start | bytes 393224 | tf_op jit(solution)/shard_map/ppermute | solution.py:680
  48.1 1.3 %collective-permute-start.5 = (f32[2,128,128]{2,1,0:T(8,128)S(1)}, f32[2,128,128]{2,1,0:T(8,128)S(1)}, u32[]{:S(2)}, u32[]{:S(2)}) collective-permute-start(f32[2,128,128]{2,1,0:T(8,128)S(1)} %get-tuple-element.133), channel_id=1, source_target_pairs={{0,4},{1,5},{2,6},{3,7},{16,20},{17,21},{18,22},{19,23}} | collective-permute-start | bytes 393224 | tf_op jit(solution)/shard_map/ppermute | solution.py:680
  49.4 3.4 %reads.4 = (bf16[4,256,128]{2,1,0:T(8,128)(2,1)S(1)}, bf16[4,256,128]{2,1,0:T(8,128)(2,1)S(1)}, f32[4,256,128]{2,1,0:T(8,128)S(1)}, s32[8,128]{1,0:T(8,128)S(1)}) custom-call(s32[8]{0:T(128)S(1)} %get-tuple-element.90.flags_ref, bf16[256,2048]{1,0:T(8,128)(2,1)S(1)} %get-tuple-element.91.query_ref, bf16[9,2048]{1,0:T(8,128)(2,1)S(1)} %collective-permute-done.tail_ref, ...), custom_call_target="tpu_custom_call" | custom-call | tf_op jit(solution)/shard_map/reads/pallas_call | solution.py:504
  52.9 0.9 %collective-permute-done.4.refs_2_ = f32[2,128,128]{2,1,0:T(8,128)S(1)} collective-permute-done((f32[2,128,128]{2,1,0:T(8,128)S(1)}, f32[2,128,128]{2,1,0:T(8,128)S(1)}, u32[]{:S(2)}, u32[]{:S(2)}) %collective-permute-start.4) | collective-permute-done | bytes 131104 | tf_op jit(solution)/shard_map/ppermute | solution.py:680
  53.8 0.7 apply.4
  54.6 1.3 %collective-permute-start.6 = (f32[2,128,128]{2,1,0:T(8,128)S(1)}, f32[2,128,128]{2,1,0:T(8,128)S(1)}, u32[]{:S(2)}, u32[]{:S(2)}) collective-permute-start(f32[2,128,128]{2,1,0:T(8,128)S(1)} %get-tuple-element.137), channel_id=1, source_target_pairs={{4,8},{5,9},{6,10},{7,11},{20,24},{21,25},{22,26},{23,27}} | collective-permute-start | bytes 393224 | tf_op jit(solution)/shard_map/ppermute | solution.py:680
  55.9 0.8 collective-permute-done.5.refs_2_
  56.6 0.7 apply.5
  57.4 1.5 %collective-permute-start.7 = (f32[2,128,128]{2,1,0:T(8,128)S(1)}, f32[2,128,128]{2,1,0:T(8,128)S(1)}, u32[]{:S(2)}, u32[]{:S(2)}) collective-permute-start(f32[2,128,128]{2,1,0:T(8,128)S(1)} %get-tuple-element.140), channel_id=1, source_target_pairs={{4,8},{5,9},{6,10},{7,11},{20,24},{21,25},{22,26},{23,27}} | collective-permute-start | bytes 393224 | tf_op jit(solution)/shard_map/ppermute | solution.py:680
  58.9 3.5 %reads.5 = (bf16[4,256,128]{2,1,0:T(8,128)(2,1)S(1)}, bf16[4,256,128]{2,1,0:T(8,128)(2,1)S(1)}, f32[4,256,128]{2,1,0:T(8,128)S(1)}, s32[8,128]{1,0:T(8,128)S(1)}) custom-call(s32[8]{0:T(128)S(1)} %get-tuple-element.90.flags_ref, bf16[256,2048]{1,0:T(8,128)(2,1)S(1)} %get-tuple-element.91.query_ref, bf16[9,2048]{1,0:T(8,128)(2,1)S(1)} %collective-permute-done.tail_ref, ...), custom_call_target="tpu_custom_call" | custom-call | tf_op jit(solution)/shard_map/reads/pallas_call | solution.py:504
  62.4 0.0 collective-permute-done.6.refs_2_
  62.4 0.8 apply.6
  63.1 0.7 collective-permute-start.8
  63.8 0.0 collective-permute-done.7.refs_2_
  63.8 0.8 apply.7
  64.6 0.7 collective-permute-start.9
  65.3 3.5 %reads.6 = (bf16[4,256,128]{2,1,0:T(8,128)(2,1)S(1)}, bf16[4,256,128]{2,1,0:T(8,128)(2,1)S(1)}, f32[4,256,128]{2,1,0:T(8,128)S(1)}, s32[8,128]{1,0:T(8,128)S(1)}) custom-call(s32[8]{0:T(128)S(1)} %get-tuple-element.90.flags_ref, bf16[256,2048]{1,0:T(8,128)(2,1)S(1)} %get-tuple-element.91.query_ref, bf16[9,2048]{1,0:T(8,128)(2,1)S(1)} %collective-permute-done.tail_ref, ...), custom_call_target="tpu_custom_call" | custom-call | tf_op jit(solution)/shard_map/reads/pallas_call | solution.py:504
  68.7 0.0 collective-permute-done.8.refs_6_
  68.7 0.0 collective-permute-done.9.refs_7_
  68.7 1.0 %fork.1 = (f32[4,128,128]{2,1,0:T(8,128)S(1)}, f32[4,128,128]{2,1,0:T(8,128)S(1)}, f32[4,128,128]{2,1,0:T(8,128)S(1)}, s32[8,128]{1,0:T(8,128)S(1)}) custom-call(s32[8]{0:T(128)S(1)} %get-tuple-element.90.flags_ref, s32[8,128]{1,0:T(8,128)S(1)} %get-tuple-element.142.token_ref, f32[4,128,256]{2,1,0:T(8,128)S(1)} %get-tuple-element.143.refs_0_, ...), custom_call_target="tpu_custom_call" | custom-call | tf_op jit(solution)/shard_map/fork/pallas_call | solution.py:545
  69.8 0.9 %collective-permute-start.10 = (f32[4,128,128]{2,1,0:T(8,128)S(1)}, f32[4,128,128]{2,1,0:T(8,128)S(1)}, u32[]{:S(2)}, u32[]{:S(2)}) collective-permute-start(f32[4,128,128]{2,1,0:T(8,128)S(1)} %get-tuple-element.158), channel_id=1, source_target_pairs={{0,1},{1,0},{2,3},{3,2},{4,5},{5,4},{6,7},{7,6},{8,9},{9,8},{10,11... | collective-permute-start | bytes 786440 | tf_op jit(solution)/shard_map/ppermute | solution.py:680
  70.6 0.2 collective-permute-start.11
  70.9 3.4 %reads.7 = (bf16[4,256,128]{2,1,0:T(8,128)(2,1)S(1)}, bf16[4,256,128]{2,1,0:T(8,128)(2,1)S(1)}, f32[4,256,128]{2,1,0:T(8,128)S(1)}, s32[8,128]{1,0:T(8,128)S(1)}) custom-call(s32[8]{0:T(128)S(1)} %get-tuple-element.90.flags_ref, bf16[256,2048]{1,0:T(8,128)(2,1)S(1)} %get-tuple-element.91.query_ref, bf16[9,2048]{1,0:T(8,128)(2,1)S(1)} %collective-permute-done.tail_ref, ...), custom_call_target="tpu_custom_call" | custom-call | tf_op jit(solution)/shard_map/reads/pallas_call | solution.py:504
  74.3 1.6 %finish.4 = (bf16[256,2048]{1,0:T(8,128)(2,1)}, s32[8,128]{1,0:T(8,128)S(1)}) custom-call(s32[8]{0:T(128)S(1)} %get-tuple-element.90.flags_ref, s32[8,128]{1,0:T(8,128)S(1)} %get-tuple-element.149.token_ref, bf16[4,256,128]{2,1,0:T(8,128)(2,1)S(1)} %get-tuple-element.150.qh_ref, bf16[4,256,128]{2,1,0:T(8,128)(2,1)S(1)} %get-tuple-element.151.ql_ref, ...), custom_call_target="tpu_custom_call" | custom-call | tf_op jit(solution)/shard_map/finish/pallas_call | solution.py:664
  75.9 1.6 %finish.5 = (bf16[256,2048]{1,0:T(8,128)(2,1)}, s32[8,128]{1,0:T(8,128)S(1)}) custom-call(s32[8]{0:T(128)S(1)} %get-tuple-element.90.flags_ref, s32[8,128]{1,0:T(8,128)S(1)} %get-tuple-element.154.token_ref, bf16[4,256,128]{2,1,0:T(8,128)(2,1)S(1)} %get-tuple-element.155.qh_ref, ...), custom_call_target="tpu_custom_call", output_to_operand_aliasing={{0}: (6, {})} | custom-call | tf_op jit(solution)/shard_map/finish/pallas_call | solution.py:664
  77.5 1.0 %collective-permute-done.11.refs_2_ = f32[4,128,128]{2,1,0:T(8,128)S(1)} collective-permute-done((f32[4,128,128]{2,1,0:T(8,128)S(1)}, f32[4,128,128]{2,1,0:T(8,128)S(1)}, u32[]{:S(2)}, u32[]{:S(2)}) %collective-permute-start.11) | collective-permute-done | bytes 262176 | tf_op jit(solution)/shard_map/ppermute | solution.py:680
  78.5 0.8 branch.1
  79.3 0.9 %collective-permute-start.12 = (f32[4,128,128]{2,1,0:T(8,128)S(1)}, f32[4,128,128]{2,1,0:T(8,128)S(1)}, u32[]{:S(2)}, u32[]{:S(2)}) collective-permute-start(f32[4,128,128]{2,1,0:T(8,128)S(1)} %get-tuple-element.172), channel_id=1, source_target_pairs={{0,1},{1,0},{2,3},{3,2},{4,5},{5,4},{6,7},{7,6},{8,9},{9,8},{10,11... | collective-permute-start | bytes 786440 | tf_op jit(solution)/shard_map/ppermute | solution.py:680
  80.2 1.6 %finish.6 = (bf16[256,2048]{1,0:T(8,128)(2,1)}, s32[8,128]{1,0:T(8,128)S(1)}) custom-call(s32[8]{0:T(128)S(1)} %get-tuple-element.90.flags_ref, s32[8,128]{1,0:T(8,128)S(1)} %get-tuple-element.162.token_ref, bf16[4,256,128]{2,1,0:T(8,128)(2,1)S(1)} %get-tuple-element.163.qh_ref, ...), custom_call_target="tpu_custom_call", output_to_operand_aliasing={{0}: (6, {})} | custom-call | tf_op jit(solution)/shard_map/finish/pallas_call | solution.py:664
  81.9 1.6 %finish.7 = (bf16[256,2048]{1,0:T(8,128)(2,1)}, s32[8,128]{1,0:T(8,128)}) custom-call(s32[8]{0:T(128)S(1)} %get-tuple-element.90.flags_ref, s32[8,128]{1,0:T(8,128)S(1)} %get-tuple-element.168.token_ref, bf16[4,256,128]{2,1,0:T(8,128)(2,1)S(1)} %get-tuple-element.169.qh_ref, ...), custom_call_target="tpu_custom_call", output_to_operand_aliasing={{0}: (6, {})} | custom-call | tf_op jit(solution)/shard_map/finish/pallas_call | solution.py:664
  (12 shorter events, 0.0 us)
Async XLA Ops:
  0.0 4.7 %copy-start.5 = (s32[8,4]{0,1:T(4,128)S(1)}, s32[8,4]{0,1:T(4,128)}, u32[]{:S(2)}) copy-start(s32[8,4]{0,1:T(4,128)} %param.14) | copy-start | bytes 388
  0.0 4.7 %copy-start.4 = (f32[256,16]{0,1:T(8,128)S(1)}, f32[256,16]{0,1:T(8,128)}, u32[]{:S(2)}) copy-start(f32[256,16]{0,1:T(8,128)} %param.13) | copy-start | bytes 49156
  0.0 4.7 %copy-start.3 = (f32[512,16]{0,1:T(8,128)S(1)}, f32[512,16]{0,1:T(8,128)}, u32[]{:S(2)}) copy-start(f32[512,16]{0,1:T(8,128)} %param.12) | copy-start | bytes 98308
  1.0 7.0 %collective-permute-start = (bf16[9,2048]{1,0:T(8,128)(2,1)S(1)}, bf16[9,2048]{1,0:T(8,128)(2,1)S(1)}, u32[]{:S(2)}, u32[]{:S(2)}) collective-permute-start(bf16[9,2048]{1,0:T(8,128)(2,1)S(1)} %last_rows.1), channel_id=1, source_target_pairs={{0,1},{1,2},{2,3},{3,4},{4,5},{5,6},{6,7},{7,8},{8,9},{9,10},{10,1... | collective-permute-start | bytes 110600 | tf_op jit(solution)/shard_map/ppermute | solution.py:680
  4.7 3.2 %copy-start = (f32[4,2048]{1,0:T(4,128)S(1)}, f32[4,2048]{1,0:T(4,128)}, u32[]{:S(2)}) copy-start(f32[4,2048]{1,0:T(4,128)} %key_kernel_ref.15) | copy-start | bytes 98308
  4.7 3.2 %copy-start.1 = (f32[4,2048]{1,0:T(4,128)S(1)}, f32[4,2048]{1,0:T(4,128)}, u32[]{:S(2)}) copy-start(f32[4,2048]{1,0:T(4,128)} %value_kernel_ref.7) | copy-start | bytes 98308
  16.6 8.8 %collective-permute-start.1 = (f32[4,128,256]{2,1,0:T(8,128)S(1)}, f32[4,128,256]{2,1,0:T(8,128)S(1)}, u32[]{:S(2)}, u32[]{:S(2)}) collective-permute-start(f32[4,128,256]{2,1,0:T(8,128)S(1)} %get-tuple-element.102), channel_id=1, source_target_pairs={{0,1},{1,0},{2,3},{3,2},{4,5},{5,4},{6,7},{7,6},{8,9},{9,8},{10,11... | collective-permute-start | bytes 1572872 | tf_op jit(solution)/shard_map/ppermute | solution.py:680
  26.3 19.4 %collective-permute-start.3 = (f32[4,128,256]{2,1,0:T(8,128)S(1)}, f32[4,128,256]{2,1,0:T(8,128)S(1)}, u32[]{:S(2)}, u32[]{:S(2)}) collective-permute-start(f32[4,128,256]{2,1,0:T(8,128)S(1)} %get-tuple-element.124), channel_id=1, source_target_pairs={{0,2},{1,3},{2,0},{3,1},{4,6},{5,7},{6,4},{7,5},{8,10},{9,11},{10,... | collective-permute-start | bytes 1572872 | tf_op jit(solution)/shard_map/ppermute | solution.py:680
  36.2 9.4 %collective-permute-start.2 = (f32[4,128,256]{2,1,0:T(8,128)S(1)}, f32[4,128,256]{2,1,0:T(8,128)S(1)}, u32[]{:S(2)}, u32[]{:S(2)}) collective-permute-start(f32[4,128,256]{2,1,0:T(8,128)S(1)} %get-tuple-element.123), channel_id=1, source_target_pairs={{0,1},{1,0},{2,3},{3,2},{4,5},{5,4},{6,7},{7,6},{8,9},{9,8},{10,11... | collective-permute-start | bytes 1572872 | tf_op jit(solution)/shard_map/ppermute | solution.py:680
  37.1 12.4 %copy-start.2 = (f32[4,2048]{1,0:T(4,128)S(1)}, f32[4,2048]{1,0:T(4,128)}, u32[]{:S(2)}) copy-start(f32[4,2048]{1,0:T(4,128)} %query_kernel_ref.7) | copy-start | bytes 98308
  46.8 7.0 %collective-permute-start.4 = (f32[2,128,128]{2,1,0:T(8,128)S(1)}, f32[2,128,128]{2,1,0:T(8,128)S(1)}, u32[]{:S(2)}, u32[]{:S(2)}) collective-permute-start(f32[2,128,128]{2,1,0:T(8,128)S(1)} %get-tuple-element.129), channel_id=1, source_target_pairs={{0,4},{1,5},{2,6},{3,7},{16,20},{17,21},{18,22},{19,23}} | collective-permute-start | bytes 393224 | tf_op jit(solution)/shard_map/ppermute | solution.py:680
  48.1 8.5 %collective-permute-start.5 = (f32[2,128,128]{2,1,0:T(8,128)S(1)}, f32[2,128,128]{2,1,0:T(8,128)S(1)}, u32[]{:S(2)}, u32[]{:S(2)}) collective-permute-start(f32[2,128,128]{2,1,0:T(8,128)S(1)} %get-tuple-element.133), channel_id=1, source_target_pairs={{0,4},{1,5},{2,6},{3,7},{16,20},{17,21},{18,22},{19,23}} | collective-permute-start | bytes 393224 | tf_op jit(solution)/shard_map/ppermute | solution.py:680
  54.6 7.8 %collective-permute-start.6 = (f32[2,128,128]{2,1,0:T(8,128)S(1)}, f32[2,128,128]{2,1,0:T(8,128)S(1)}, u32[]{:S(2)}, u32[]{:S(2)}) collective-permute-start(f32[2,128,128]{2,1,0:T(8,128)S(1)} %get-tuple-element.137), channel_id=1, source_target_pairs={{4,8},{5,9},{6,10},{7,11},{20,24},{21,25},{22,26},{23,27}} | collective-permute-start | bytes 393224 | tf_op jit(solution)/shard_map/ppermute | solution.py:680
  57.4 6.4 %collective-permute-start.7 = (f32[2,128,128]{2,1,0:T(8,128)S(1)}, f32[2,128,128]{2,1,0:T(8,128)S(1)}, u32[]{:S(2)}, u32[]{:S(2)}) collective-permute-start(f32[2,128,128]{2,1,0:T(8,128)S(1)} %get-tuple-element.140), channel_id=1, source_target_pairs={{4,8},{5,9},{6,10},{7,11},{20,24},{21,25},{22,26},{23,27}} | collective-permute-start | bytes 393224 | tf_op jit(solution)/shard_map/ppermute | solution.py:680
  63.1 5.6 %collective-permute-start.8 = (f32[2,128,128]{2,1,0:T(8,128)S(1)}, f32[2,128,128]{2,1,0:T(8,128)S(1)}, u32[]{:S(2)}, u32[]{:S(2)}) collective-permute-start(f32[2,128,128]{2,1,0:T(8,128)S(1)} %get-tuple-element.146), channel_id=1, source_target_pairs={{8,12},{9,13},{10,14},{11,15},{24,28},{25,29},{26,30},{27,31}} | collective-permute-start | bytes 393224 | tf_op jit(solution)/shard_map/ppermute | solution.py:680
  64.6 4.1 %collective-permute-start.9 = (f32[2,128,128]{2,1,0:T(8,128)S(1)}, f32[2,128,128]{2,1,0:T(8,128)S(1)}, u32[]{:S(2)}, u32[]{:S(2)}) collective-permute-start(f32[2,128,128]{2,1,0:T(8,128)S(1)} %get-tuple-element.147), channel_id=1, source_target_pairs={{8,12},{9,13},{10,14},{11,15},{24,28},{25,29},{26,30},{27,31}} | collective-permute-start | bytes 393224 | tf_op jit(solution)/shard_map/ppermute | solution.py:680
  69.8 6.2 %collective-permute-start.10 = (f32[4,128,128]{2,1,0:T(8,128)S(1)}, f32[4,128,128]{2,1,0:T(8,128)S(1)}, u32[]{:S(2)}, u32[]{:S(2)}) collective-permute-start(f32[4,128,128]{2,1,0:T(8,128)S(1)} %get-tuple-element.158), channel_id=1, source_target_pairs={{0,1},{1,0},{2,3},{3,2},{4,5},{5,4},{6,7},{7,6},{8,9},{9,8},{10,11... | collective-permute-start | bytes 786440 | tf_op jit(solution)/shard_map/ppermute | solution.py:680
  70.6 7.9 %collective-permute-start.11 = (f32[4,128,128]{2,1,0:T(8,128)S(1)}, f32[4,128,128]{2,1,0:T(8,128)S(1)}, u32[]{:S(2)}, u32[]{:S(2)}) collective-permute-start(f32[4,128,128]{2,1,0:T(8,128)S(1)} %get-tuple-element.161), channel_id=1, source_target_pairs={{0,2},{1,3},{2,0},{3,1},{4,6},{5,7},{6,4},{7,5},{8,10},{9,11},{10,... | collective-permute-start | bytes 786440 | tf_op jit(solution)/shard_map/ppermute | solution.py:680
  79.3 2.5 %collective-permute-start.12 = (f32[4,128,128]{2,1,0:T(8,128)S(1)}, f32[4,128,128]{2,1,0:T(8,128)S(1)}, u32[]{:S(2)}, u32[]{:S(2)}) collective-permute-start(f32[4,128,128]{2,1,0:T(8,128)S(1)} %get-tuple-element.172), channel_id=1, source_target_pairs={{0,1},{1,0},{2,3},{3,2},{4,5},{5,4},{6,7},{7,6},{8,9},{9,8},{10,11... | collective-permute-start | bytes 786440 | tf_op jit(solution)/shard_map/ppermute | solution.py:680
where the time goes:
time: 83.7 us; the launch traced here: 83.5 us
  Pallas kernels  65.7 us (78%)
  starting transfers between devices  14.7 us (18%)
  waiting for transfers between devices  2.69 us (3%)
    pallas_call x4, Pallas kernels, group_maps(): pl.pallas_call(functools.partial(maps_kernel, which), grid_spec=pltpu.Pre...  34.5 us
    ppermute x13, starting transfers between devices, moved(): lax.ppermute(x, 'seq', pairs)  14.7 us
    pallas_call x4, Pallas kernels, group_reads(): pl.pallas_call(functools.partial(reads_kernel, which), grid_spec=pltpu.Pr...  13.8 us
    pallas_call x8, Pallas kernels, small(): pl.pallas_call(body, grid_spec=pltpu.PrefetchScalarGridSpec(num_scalar_pr...  6.83 us
    pallas_call x4, Pallas kernels, finished(): pl.pallas_call(finish_kernel, grid_spec=pltpu.PrefetchScalarGridSpec(num_...  6.47 us
    pallas_call x1, Pallas kernels, prep(): pl.pallas_call(prep_kernel, out_shape=(jax.ShapeDtypeStruct((PLANE, steps...  3.18 us
    ppermute x13, waiting for transfers between devices, moved(): lax.ppermute(x, 'seq', pairs)  2.69 us
  transfers between devices with their start and end apart: 13, of which 3 were waited for; matrix products, arithmetic and copies ran while one was open for 0% of the time, Pallas kernels for 61%

commit v1 on v0

--- a/solution.py
+++ b/solution.py
@@ -647,10 +647,12 @@
 def finish_kernel(flags_ref, token_ref, qh_ref, ql_ref, own_ref, entry_ref, *refs):
     out_ref, token_out = refs[-2:]
     hand_on(token_ref, token_out)
+    count = out_ref.shape[0]
+    rows = pl.ds(pl.multiple_of(pl.program_id(0) * count, count), count)
     for h in range(entry_ref.shape[0]):
         lanes = slice(h * DK, (h + 1) * DK)
-        got = mm3((qh_ref[h], ql_ref[h]), split(entry_ref[h]))
-        out_ref[:, lanes] = (own_ref[h] + got).astype(BF16)
+        got = mm3((qh_ref[h, rows, :], ql_ref[h, rows, :]), split(entry_ref[h]))
+        out_ref[:, lanes] = (own_ref[h, rows, :] + got).astype(BF16)
 
 
 def finished(flags, token, which, read, entry, out, width):
@@ -665,9 +667,9 @@
         finish_kernel,
         grid_spec=pltpu.PrefetchScalarGridSpec(
             num_scalar_prefetch=1,
-            grid=(1,),
+            grid=(2,),
             in_specs=specs,
-            out_specs=[pl.BlockSpec((tokens, group * DK), lambda i, g: (0, g[GROUPS + which])), WHOLE],
+            out_specs=[pl.BlockSpec((tokens // 2, group * DK), lambda i, g: (i, g[GROUPS + which])), WHOLE],
         ),
         out_shape=[jax.ShapeDtypeStruct((tokens, width), BF16), TOKEN],
         input_output_aliases={} if out is None else {len(operands): 0},

time: 83.7 us -> 84 us (level)
  no operation moved by 1% of the time
where the time goes in v1:
time: 84 us; the launch traced here: 83.8 us
  Pallas kernels  66.3 us (79%)
  starting transfers between devices  14.7 us (18%)
  waiting for transfers between devices  2.41 us (3%)
    pallas_call x4, Pallas kernels, group_maps(): pl.pallas_call(functools.partial(maps_kernel, which), grid_spec=pltpu.Pre...  34.5 us
    ppermute x13, starting transfers between devices, moved(): lax.ppermute(x, 'seq', pairs)  14.7 us
    pallas_call x4, Pallas kernels, group_reads(): pl.pallas_call(functools.partial(reads_kernel, which), grid_spec=pltpu.Pr...  13.8 us
    pallas_call x4, Pallas kernels, finished(): pl.pallas_call(finish_kernel, grid_spec=pltpu.PrefetchScalarGridSpec(num_...  7.03 us
    pallas_call x8, Pallas kernels, small(): pl.pallas_call(body, grid_spec=pltpu.PrefetchScalarGridSpec(num_scalar_pr...  6.83 us
    pallas_call x1, Pallas kernels, prep(): pl.pallas_call(prep_kernel, out_shape=(jax.ShapeDtypeStruct((PLANE, steps...  3.18 us
    ppermute x13, waiting for transfers between devices, moved(): lax.ppermute(x, 'seq', pairs)  2.41 us
  transfers between devices with their start and end apart: 13, of which 3 were waited for; matrix products, arithmetic and copies ran while one was open for 0% of the time, Pallas kernels for 61%

profile of v1, /device:TPU:9, one launch (start us, length us, event | category | flops | bytes accessed | tf_op | source)
XLA Modules:
  0.0 83.8 jit_solution(3142563577432017459)
XLA Ops:
  0.0 1.0 %last_rows.1 = bf16[9,2048]{1,0:T(8,128)(2,1)S(1)} custom-call(bf16[256,2048]{1,0:T(8,128)(2,1)} %query_ref.1, bf16[512,2048]{1,0:T(8,128)(2,1)} %key_ref.1, bf16[512,2048]{1,0:T(8,128)(2,1)} %value_ref.1), custom_call_target="tpu_custom_call" | custom-call | tf_op jit(solution)/shard_map/last_rows/pallas_call | solution.py:181
  1.0 3.7 %collective-permute-start = (bf16[9,2048]{1,0:T(8,128)(2,1)S(1)}, bf16[9,2048]{1,0:T(8,128)(2,1)S(1)}, u32[]{:S(2)}, u32[]{:S(2)}) collective-permute-start(bf16[9,2048]{1,0:T(8,128)(2,1)S(1)} %last_rows.1), channel_id=1, source_target_pairs={{0,1},{1,2},{2,3},{3,4},{4,5},{5,6},{6,7},{7,8},{8,9},{9,10},{10,1... | collective-permute-start | bytes 110600 | tf_op jit(solution)/shard_map/ppermute | solution.py:682
  4.7 0.0 copy-start
  4.7 0.0 copy-start.1
  4.8 3.2 %prep.1 = (f32[4,512,4]{2,1,0:T(8,128)S(1)}, f32[4,512,4]{2,1,0:T(8,128)S(1)}, f32[16,4,128]{2,1,0:T(4,128)S(1)}, f32[4,256,4]{2,1,0:T(8,128)S(1)}, s32[8]{0:T(1...) custom-call(s32[1]{0:T(128)} %bitcast.at_ref, ...), custom_call_target="tpu_custom_call" | custom-call | tf_op jit(solution)/shard_map/prep/pallas_call | solution.py:196
  7.9 0.0 collective-permute-done.tail_ref
  8.0 8.6 %maps.4 = (f32[4,128,256]{2,1,0:T(8,128)S(1)}, bf16[4,512,256]{2,1,0:T(8,128)(2,1)S(1)}, bf16[4,512,256]{2,1,0:T(8,128)(2,1)S(1)}, bf16[4,384,256]{2,1,0:T(8,128...) custom-call(s32[8]{0:T(128)S(1)} %get-tuple-element.90.flags_ref, ...), custom_call_target="tpu_custom_call" | custom-call | tf_op jit(solution)/shard_map/maps/pallas_call | solution.py:371
  16.6 0.3 collective-permute-start.1
  16.8 8.6 %maps.5 = (f32[4,128,256]{2,1,0:T(8,128)S(1)}, bf16[4,512,256]{2,1,0:T(8,128)(2,1)S(1)}, bf16[4,512,256]{2,1,0:T(8,128)(2,1)S(1)}, bf16[4,384,256]{2,1,0:T(8,128...) custom-call(s32[8]{0:T(128)S(1)} %get-tuple-element.90.flags_ref, ...), custom_call_target="tpu_custom_call" | custom-call | tf_op jit(solution)/shard_map/maps/pallas_call | solution.py:371
  25.4 0.0 collective-permute-done.1.refs_1_
  25.4 0.9 %compose.1 = (f32[4,128,256]{2,1,0:T(8,128)S(1)}, s32[8,128]{1,0:T(8,128)S(1)}) custom-call(s32[8]{0:T(128)S(1)} %get-tuple-element.90.flags_ref, s32[8,128]{1,0:T(8,128)S(1)} %get-tuple-element.100.token_ref, f32[4,128,256]{2,1,0:T(8,128)S(1)} %get-tuple-element.101.refs_0_, f32[4,128,256]{2,1,0:T(8,128)S(1)} %collective-permute-done.1.refs_1_), custom_call_target="tpu_custom_call" | custom-call | tf_op jit(solution)/shard_map/compose/pallas_call | solution.py:545
  26.3 1.2 %collective-permute-start.3 = (f32[4,128,256]{2,1,0:T(8,128)S(1)}, f32[4,128,256]{2,1,0:T(8,128)S(1)}, u32[]{:S(2)}, u32[]{:S(2)}) collective-permute-start(f32[4,128,256]{2,1,0:T(8,128)S(1)} %get-tuple-element.124), channel_id=1, source_target_pairs={{0,2},{1,3},{2,0},{3,1},{4,6},{5,7},{6,4},{7,5},{8,10},{9,11},{10,... | collective-permute-start | bytes 1572872 | tf_op jit(solution)/shard_map/ppermute | solution.py:682
  27.5 8.8 %maps.6 = (f32[4,128,256]{2,1,0:T(8,128)S(1)}, bf16[4,512,256]{2,1,0:T(8,128)(2,1)S(1)}, bf16[4,512,256]{2,1,0:T(8,128)(2,1)S(1)}, bf16[4,384,256]{2,1,0:T(8,128...) custom-call(s32[8]{0:T(128)S(1)} %get-tuple-element.90.flags_ref, ...), custom_call_target="tpu_custom_call" | custom-call | tf_op jit(solution)/shard_map/maps/pallas_call | solution.py:371
  36.2 0.8 collective-permute-start.2
  37.1 8.6 %maps.7 = (f32[4,128,256]{2,1,0:T(8,128)S(1)}, bf16[4,512,256]{2,1,0:T(8,128)(2,1)S(1)}, bf16[4,512,256]{2,1,0:T(8,128)(2,1)S(1)}, bf16[4,384,256]{2,1,0:T(8,128...) custom-call(s32[8]{0:T(128)S(1)} %get-tuple-element.90.flags_ref, ...), custom_call_target="tpu_custom_call" | custom-call | tf_op jit(solution)/shard_map/maps/pallas_call | solution.py:371
  45.7 0.0 collective-permute-done.3.refs_2_.refs_1_
  45.7 0.0 collective-permute-done.2.refs_1_.refs_3_
  45.7 1.1 %plane.1 = (f32[4,128,256]{2,1,0:T(8,128)S(1)}, f32[2,128,256]{2,1,0:T(8,128)S(1)}, f32[2,128,256]{2,1,0:T(8,128)S(1)}, f32[2,128,128]{2,1,0:T(8,128)S(1)}, f32[...) custom-call(s32[8]{0:T(128)S(1)} %get-tuple-element.90.flags_ref, ...), custom_call_target="tpu_custom_call" | custom-call | tf_op jit(solution)/shard_map/plane/pallas_call | solution.py:545
  46.8 1.3 %collective-permute-start.4 = (f32[2,128,128]{2,1,0:T(8,128)S(1)}, f32[2,128,128]{2,1,0:T(8,128)S(1)}, u32[]{:S(2)}, u32[]{:S(2)}) collective-permute-start(f32[2,128,128]{2,1,0:T(8,128)S(1)} %get-tuple-element.129), channel_id=1, source_target_pairs={{0,4},{1,5},{2,6},{3,7},{16,20},{17,21},{18,22},{19,23}} | collective-permute-start | bytes 393224 | tf_op jit(solution)/shard_map/ppermute | solution.py:682
  48.1 1.3 %collective-permute-start.5 = (f32[2,128,128]{2,1,0:T(8,128)S(1)}, f32[2,128,128]{2,1,0:T(8,128)S(1)}, u32[]{:S(2)}, u32[]{:S(2)}) collective-permute-start(f32[2,128,128]{2,1,0:T(8,128)S(1)} %get-tuple-element.133), channel_id=1, source_target_pairs={{0,4},{1,5},{2,6},{3,7},{16,20},{17,21},{18,22},{19,23}} | collective-permute-start | bytes 393224 | tf_op jit(solution)/shard_map/ppermute | solution.py:682
  49.4 3.4 %reads.4 = (bf16[4,256,128]{2,1,0:T(8,128)(2,1)S(1)}, bf16[4,256,128]{2,1,0:T(8,128)(2,1)S(1)}, f32[4,256,128]{2,1,0:T(8,128)S(1)}, s32[8,128]{1,0:T(8,128)S(1)}) custom-call(s32[8]{0:T(128)S(1)} %get-tuple-element.90.flags_ref, bf16[256,2048]{1,0:T(8,128)(2,1)S(1)} %get-tuple-element.91.query_ref, bf16[9,2048]{1,0:T(8,128)(2,1)S(1)} %collective-permute-done.tail_ref, ...), custom_call_target="tpu_custom_call" | custom-call | tf_op jit(solution)/shard_map/reads/pallas_call | solution.py:504
  52.9 0.9 %collective-permute-done.4.refs_2_ = f32[2,128,128]{2,1,0:T(8,128)S(1)} collective-permute-done((f32[2,128,128]{2,1,0:T(8,128)S(1)}, f32[2,128,128]{2,1,0:T(8,128)S(1)}, u32[]{:S(2)}, u32[]{:S(2)}) %collective-permute-start.4) | collective-permute-done | bytes 131104 | tf_op jit(solution)/shard_map/ppermute | solution.py:682
  53.8 0.7 apply.4
  54.6 1.3 %collective-permute-start.6 = (f32[2,128,128]{2,1,0:T(8,128)S(1)}, f32[2,128,128]{2,1,0:T(8,128)S(1)}, u32[]{:S(2)}, u32[]{:S(2)}) collective-permute-start(f32[2,128,128]{2,1,0:T(8,128)S(1)} %get-tuple-element.137), channel_id=1, source_target_pairs={{4,8},{5,9},{6,10},{7,11},{20,24},{21,25},{22,26},{23,27}} | collective-permute-start | bytes 393224 | tf_op jit(solution)/shard_map/ppermute | solution.py:682
  55.9 0.8 collective-permute-done.5.refs_2_
  56.6 0.7 apply.5
  57.4 1.5 %collective-permute-start.7 = (f32[2,128,128]{2,1,0:T(8,128)S(1)}, f32[2,128,128]{2,1,0:T(8,128)S(1)}, u32[]{:S(2)}, u32[]{:S(2)}) collective-permute-start(f32[2,128,128]{2,1,0:T(8,128)S(1)} %get-tuple-element.140), channel_id=1, source_target_pairs={{4,8},{5,9},{6,10},{7,11},{20,24},{21,25},{22,26},{23,27}} | collective-permute-start | bytes 393224 | tf_op jit(solution)/shard_map/ppermute | solution.py:682
  58.9 3.5 %reads.5 = (bf16[4,256,128]{2,1,0:T(8,128)(2,1)S(1)}, bf16[4,256,128]{2,1,0:T(8,128)(2,1)S(1)}, f32[4,256,128]{2,1,0:T(8,128)S(1)}, s32[8,128]{1,0:T(8,128)S(1)}) custom-call(s32[8]{0:T(128)S(1)} %get-tuple-element.90.flags_ref, bf16[256,2048]{1,0:T(8,128)(2,1)S(1)} %get-tuple-element.91.query_ref, bf16[9,2048]{1,0:T(8,128)(2,1)S(1)} %collective-permute-done.tail_ref, ...), custom_call_target="tpu_custom_call" | custom-call | tf_op jit(solution)/shard_map/reads/pallas_call | solution.py:504
  62.4 0.8 apply.6
  63.1 0.7 collective-permute-start.8
  63.8 0.0 collective-permute-done.7.refs_2_
  63.8 0.8 apply.7
  64.6 0.7 collective-permute-start.9
  65.3 3.5 %reads.6 = (bf16[4,256,128]{2,1,0:T(8,128)(2,1)S(1)}, bf16[4,256,128]{2,1,0:T(8,128)(2,1)S(1)}, f32[4,256,128]{2,1,0:T(8,128)S(1)}, s32[8,128]{1,0:T(8,128)S(1)}) custom-call(s32[8]{0:T(128)S(1)} %get-tuple-element.90.flags_ref, bf16[256,2048]{1,0:T(8,128)(2,1)S(1)} %get-tuple-element.91.query_ref, bf16[9,2048]{1,0:T(8,128)(2,1)S(1)} %collective-permute-done.tail_ref, ...), custom_call_target="tpu_custom_call" | custom-call | tf_op jit(solution)/shard_map/reads/pallas_call | solution.py:504
  68.7 0.0 collective-permute-done.9.refs_7_
  68.7 1.0 %fork.1 = (f32[4,128,128]{2,1,0:T(8,128)S(1)}, f32[4,128,128]{2,1,0:T(8,128)S(1)}, f32[4,128,128]{2,1,0:T(8,128)S(1)}, s32[8,128]{1,0:T(8,128)S(1)}) custom-call(s32[8]{0:T(128)S(1)} %get-tuple-element.90.flags_ref, s32[8,128]{1,0:T(8,128)S(1)} %get-tuple-element.142.token_ref, f32[4,128,256]{2,1,0:T(8,128)S(1)} %get-tuple-element.143.refs_0_, ...), custom_call_target="tpu_custom_call" | custom-call | tf_op jit(solution)/shard_map/fork/pallas_call | solution.py:545
  69.8 0.9 %collective-permute-start.10 = (f32[4,128,128]{2,1,0:T(8,128)S(1)}, f32[4,128,128]{2,1,0:T(8,128)S(1)}, u32[]{:S(2)}, u32[]{:S(2)}) collective-permute-start(f32[4,128,128]{2,1,0:T(8,128)S(1)} %get-tuple-element.158), channel_id=1, source_target_pairs={{0,1},{1,0},{2,3},{3,2},{4,5},{5,4},{6,7},{7,6},{8,9},{9,8},{10,11... | collective-permute-start | bytes 786440 | tf_op jit(solution)/shard_map/ppermute | solution.py:682
  70.6 0.2 collective-permute-start.11
  70.9 3.4 %reads.7 = (bf16[4,256,128]{2,1,0:T(8,128)(2,1)S(1)}, bf16[4,256,128]{2,1,0:T(8,128)(2,1)S(1)}, f32[4,256,128]{2,1,0:T(8,128)S(1)}, s32[8,128]{1,0:T(8,128)S(1)}) custom-call(s32[8]{0:T(128)S(1)} %get-tuple-element.90.flags_ref, bf16[256,2048]{1,0:T(8,128)(2,1)S(1)} %get-tuple-element.91.query_ref, bf16[9,2048]{1,0:T(8,128)(2,1)S(1)} %collective-permute-done.tail_ref, ...), custom_call_target="tpu_custom_call" | custom-call | tf_op jit(solution)/shard_map/reads/pallas_call | solution.py:504
  74.3 1.8 %finish.4 = (bf16[256,2048]{1,0:T(8,128)(2,1)}, s32[8,128]{1,0:T(8,128)S(1)}) custom-call(s32[8]{0:T(128)S(1)} %get-tuple-element.90.flags_ref, s32[8,128]{1,0:T(8,128)S(1)} %get-tuple-element.149.token_ref, bf16[4,256,128]{2,1,0:T(8,128)(2,1)S(1)} %get-tuple-element.150.qh_ref, bf16[4,256,128]{2,1,0:T(8,128)(2,1)S(1)} %get-tuple-element.151.ql_ref, ...), custom_call_target="tpu_custom_call" | custom-call | tf_op jit(solution)/shard_map/finish/pallas_call | solution.py:666
  76.1 0.0 collective-permute-done.10.entry_ref
  76.1 1.8 %finish.5 = (bf16[256,2048]{1,0:T(8,128)(2,1)}, s32[8,128]{1,0:T(8,128)S(1)}) custom-call(s32[8]{0:T(128)S(1)} %get-tuple-element.90.flags_ref, s32[8,128]{1,0:T(8,128)S(1)} %get-tuple-element.154.token_ref, bf16[4,256,128]{2,1,0:T(8,128)(2,1)S(1)} %get-tuple-element.155.qh_ref, ...), custom_call_target="tpu_custom_call", output_to_operand_aliasing={{0}: (6, {})} | custom-call | tf_op jit(solution)/shard_map/finish/pallas_call | solution.py:666
  77.8 0.7 collective-permute-done.11.refs_2_
  78.5 0.8 branch.1
  79.3 0.9 %collective-permute-start.12 = (f32[4,128,128]{2,1,0:T(8,128)S(1)}, f32[4,128,128]{2,1,0:T(8,128)S(1)}, u32[]{:S(2)}, u32[]{:S(2)}) collective-permute-start(f32[4,128,128]{2,1,0:T(8,128)S(1)} %get-tuple-element.172), channel_id=1, source_target_pairs={{0,1},{1,0},{2,3},{3,2},{4,5},{5,4},{6,7},{7,6},{8,9},{9,8},{10,11... | collective-permute-start | bytes 786440 | tf_op jit(solution)/shard_map/ppermute | solution.py:682
  80.2 1.8 %finish.6 = (bf16[256,2048]{1,0:T(8,128)(2,1)}, s32[8,128]{1,0:T(8,128)S(1)}) custom-call(s32[8]{0:T(128)S(1)} %get-tuple-element.90.flags_ref, s32[8,128]{1,0:T(8,128)S(1)} %get-tuple-element.162.token_ref, bf16[4,256,128]{2,1,0:T(8,128)(2,1)S(1)} %get-tuple-element.163.qh_ref, ...), custom_call_target="tpu_custom_call", output_to_operand_aliasing={{0}: (6, {})} | custom-call | tf_op jit(solution)/shard_map/finish/pallas_call | solution.py:666
  82.0 0.0 collective-permute-done.12.entry_ref
  82.0 1.8 %finish.7 = (bf16[256,2048]{1,0:T(8,128)(2,1)}, s32[8,128]{1,0:T(8,128)}) custom-call(s32[8]{0:T(128)S(1)} %get-tuple-element.90.flags_ref, s32[8,128]{1,0:T(8,128)S(1)} %get-tuple-element.168.token_ref, bf16[4,256,128]{2,1,0:T(8,128)(2,1)S(1)} %get-tuple-element.169.qh_ref, ...), custom_call_target="tpu_custom_call", output_to_operand_aliasing={{0}: (6, {})} | custom-call | tf_op jit(solution)/shard_map/finish/pallas_call | solution.py:666
  (12 shorter events, 0.0 us)
Async XLA Ops:
  0.0 4.7 %copy-start.5 = (s32[8,4]{0,1:T(4,128)S(1)}, s32[8,4]{0,1:T(4,128)}, u32[]{:S(2)}) copy-start(s32[8,4]{0,1:T(4,128)} %param.14) | copy-start | bytes 388
  0.0 4.7 %copy-start.4 = (f32[256,16]{0,1:T(8,128)S(1)}, f32[256,16]{0,1:T(8,128)}, u32[]{:S(2)}) copy-start(f32[256,16]{0,1:T(8,128)} %param.13) | copy-start | bytes 49156
  0.0 4.7 %copy-start.3 = (f32[512,16]{0,1:T(8,128)S(1)}, f32[512,16]{0,1:T(8,128)}, u32[]{:S(2)}) copy-start(f32[512,16]{0,1:T(8,128)} %param.12) | copy-start | bytes 98308
  1.0 7.0 %collective-permute-start = (bf16[9,2048]{1,0:T(8,128)(2,1)S(1)}, bf16[9,2048]{1,0:T(8,128)(2,1)S(1)}, u32[]{:S(2)}, u32[]{:S(2)}) collective-permute-start(bf16[9,2048]{1,0:T(8,128)(2,1)S(1)} %last_rows.1), channel_id=1, source_target_pairs={{0,1},{1,2},{2,3},{3,4},{4,5},{5,6},{6,7},{7,8},{8,9},{9,10},{10,1... | collective-permute-start | bytes 110600 | tf_op jit(solution)/shard_map/ppermute | solution.py:682
  4.7 3.2 %copy-start = (f32[4,2048]{1,0:T(4,128)S(1)}, f32[4,2048]{1,0:T(4,128)}, u32[]{:S(2)}) copy-start(f32[4,2048]{1,0:T(4,128)} %key_kernel_ref.15) | copy-start | bytes 98308
  4.7 3.2 %copy-start.1 = (f32[4,2048]{1,0:T(4,128)S(1)}, f32[4,2048]{1,0:T(4,128)}, u32[]{:S(2)}) copy-start(f32[4,2048]{1,0:T(4,128)} %value_kernel_ref.7) | copy-start | bytes 98308
  16.6 8.8 %collective-permute-start.1 = (f32[4,128,256]{2,1,0:T(8,128)S(1)}, f32[4,128,256]{2,1,0:T(8,128)S(1)}, u32[]{:S(2)}, u32[]{:S(2)}) collective-permute-start(f32[4,128,256]{2,1,0:T(8,128)S(1)} %get-tuple-element.102), channel_id=1, source_target_pairs={{0,1},{1,0},{2,3},{3,2},{4,5},{5,4},{6,7},{7,6},{8,9},{9,8},{10,11... | collective-permute-start | bytes 1572872 | tf_op jit(solution)/shard_map/ppermute | solution.py:682
  26.3 19.4 %collective-permute-start.3 = (f32[4,128,256]{2,1,0:T(8,128)S(1)}, f32[4,128,256]{2,1,0:T(8,128)S(1)}, u32[]{:S(2)}, u32[]{:S(2)}) collective-permute-start(f32[4,128,256]{2,1,0:T(8,128)S(1)} %get-tuple-element.124), channel_id=1, source_target_pairs={{0,2},{1,3},{2,0},{3,1},{4,6},{5,7},{6,4},{7,5},{8,10},{9,11},{10,... | collective-permute-start | bytes 1572872 | tf_op jit(solution)/shard_map/ppermute | solution.py:682
  36.2 9.4 %collective-permute-start.2 = (f32[4,128,256]{2,1,0:T(8,128)S(1)}, f32[4,128,256]{2,1,0:T(8,128)S(1)}, u32[]{:S(2)}, u32[]{:S(2)}) collective-permute-start(f32[4,128,256]{2,1,0:T(8,128)S(1)} %get-tuple-element.123), channel_id=1, source_target_pairs={{0,1},{1,0},{2,3},{3,2},{4,5},{5,4},{6,7},{7,6},{8,9},{9,8},{10,11... | collective-permute-start | bytes 1572872 | tf_op jit(solution)/shard_map/ppermute | solution.py:682
  37.1 12.4 %copy-start.2 = (f32[4,2048]{1,0:T(4,128)S(1)}, f32[4,2048]{1,0:T(4,128)}, u32[]{:S(2)}) copy-start(f32[4,2048]{1,0:T(4,128)} %query_kernel_ref.7) | copy-start | bytes 98308
  46.8 7.0 %collective-permute-start.4 = (f32[2,128,128]{2,1,0:T(8,128)S(1)}, f32[2,128,128]{2,1,0:T(8,128)S(1)}, u32[]{:S(2)}, u32[]{:S(2)}) collective-permute-start(f32[2,128,128]{2,1,0:T(8,128)S(1)} %get-tuple-element.129), channel_id=1, source_target_pairs={{0,4},{1,5},{2,6},{3,7},{16,20},{17,21},{18,22},{19,23}} | collective-permute-start | bytes 393224 | tf_op jit(solution)/shard_map/ppermute | solution.py:682
  48.1 8.5 %collective-permute-start.5 = (f32[2,128,128]{2,1,0:T(8,128)S(1)}, f32[2,128,128]{2,1,0:T(8,128)S(1)}, u32[]{:S(2)}, u32[]{:S(2)}) collective-permute-start(f32[2,128,128]{2,1,0:T(8,128)S(1)} %get-tuple-element.133), channel_id=1, source_target_pairs={{0,4},{1,5},{2,6},{3,7},{16,20},{17,21},{18,22},{19,23}} | collective-permute-start | bytes 393224 | tf_op jit(solution)/shard_map/ppermute | solution.py:682
  54.6 7.8 %collective-permute-start.6 = (f32[2,128,128]{2,1,0:T(8,128)S(1)}, f32[2,128,128]{2,1,0:T(8,128)S(1)}, u32[]{:S(2)}, u32[]{:S(2)}) collective-permute-start(f32[2,128,128]{2,1,0:T(8,128)S(1)} %get-tuple-element.137), channel_id=1, source_target_pairs={{4,8},{5,9},{6,10},{7,11},{20,24},{21,25},{22,26},{23,27}} | collective-permute-start | bytes 393224 | tf_op jit(solution)/shard_map/ppermute | solution.py:682
  57.4 6.4 %collective-permute-start.7 = (f32[2,128,128]{2,1,0:T(8,128)S(1)}, f32[2,128,128]{2,1,0:T(8,128)S(1)}, u32[]{:S(2)}, u32[]{:S(2)}) collective-permute-start(f32[2,128,128]{2,1,0:T(8,128)S(1)} %get-tuple-element.140), channel_id=1, source_target_pairs={{4,8},{5,9},{6,10},{7,11},{20,24},{21,25},{22,26},{23,27}} | collective-permute-start | bytes 393224 | tf_op jit(solution)/shard_map/ppermute | solution.py:682
  63.1 5.6 %collective-permute-start.8 = (f32[2,128,128]{2,1,0:T(8,128)S(1)}, f32[2,128,128]{2,1,0:T(8,128)S(1)}, u32[]{:S(2)}, u32[]{:S(2)}) collective-permute-start(f32[2,128,128]{2,1,0:T(8,128)S(1)} %get-tuple-element.146), channel_id=1, source_target_pairs={{8,12},{9,13},{10,14},{11,15},{24,28},{25,29},{26,30},{27,31}} | collective-permute-start | bytes 393224 | tf_op jit(solution)/shard_map/ppermute | solution.py:682
  64.6 4.1 %collective-permute-start.9 = (f32[2,128,128]{2,1,0:T(8,128)S(1)}, f32[2,128,128]{2,1,0:T(8,128)S(1)}, u32[]{:S(2)}, u32[]{:S(2)}) collective-permute-start(f32[2,128,128]{2,1,0:T(8,128)S(1)} %get-tuple-element.147), channel_id=1, source_target_pairs={{8,12},{9,13},{10,14},{11,15},{24,28},{25,29},{26,30},{27,31}} | collective-permute-start | bytes 393224 | tf_op jit(solution)/shard_map/ppermute | solution.py:682
  69.8 6.3 %collective-permute-start.10 = (f32[4,128,128]{2,1,0:T(8,128)S(1)}, f32[4,128,128]{2,1,0:T(8,128)S(1)}, u32[]{:S(2)}, u32[]{:S(2)}) collective-permute-start(f32[4,128,128]{2,1,0:T(8,128)S(1)} %get-tuple-element.158), channel_id=1, source_target_pairs={{0,1},{1,0},{2,3},{3,2},{4,5},{5,4},{6,7},{7,6},{8,9},{9,8},{10,11... | collective-permute-start | bytes 786440 | tf_op jit(solution)/shard_map/ppermute | solution.py:682
  70.6 7.9 %collective-permute-start.11 = (f32[4,128,128]{2,1,0:T(8,128)S(1)}, f32[4,128,128]{2,1,0:T(8,128)S(1)}, u32[]{:S(2)}, u32[]{:S(2)}) collective-permute-start(f32[4,128,128]{2,1,0:T(8,128)S(1)} %get-tuple-element.161), channel_id=1, source_target_pairs={{0,2},{1,3},{2,0},{3,1},{4,6},{5,7},{6,4},{7,5},{8,10},{9,11},{10,... | collective-permute-start | bytes 786440 | tf_op jit(solution)/shard_map/ppermute | solution.py:682
  79.3 2.7 %collective-permute-start.12 = (f32[4,128,128]{2,1,0:T(8,128)S(1)}, f32[4,128,128]{2,1,0:T(8,128)S(1)}, u32[]{:S(2)}, u32[]{:S(2)}) collective-permute-start(f32[4,128,128]{2,1,0:T(8,128)S(1)} %get-tuple-element.172), channel_id=1, source_target_pairs={{0,1},{1,0},{2,3},{3,2},{4,5},{5,4},{6,7},{7,6},{8,9},{9,8},{10,11... | collective-permute-start | bytes 786440 | tf_op jit(solution)/shard_map/ppermute | solution.py:682
